TPU v7x, 128 devices: a whole 4x4x4 slice. The times are simulated.
128 devices in a mesh: batch: 4 (over z), head: 2 (over core), seq: 16 (over x, y).
Axes of the slice: x: 4, y: 4, z: 4, core: 2. Of those that a mesh axis runs over, the one named last changes fastest.
Arguments:
- hidden: float32 [32768, 8192], P(('batch', 'seq')), parts along dimension 0, may hold values from -6 to 6
- row_scale: float32 [32768], P(('batch', 'seq')), parts along dimension 0, may hold values from 0.25 to 4
- key_value_weight: float32 [8192, 8, 256], P('seq', 'head'), may hold values from -0.0625 to 0.0625
- outlier: int32 [512, 8], P(('batch', 'seq'), 'head'), parts along dimension 0, may hold values 0 or 1
- sketch_sign_flags: int32 [8, 2, 128, 64], P('head'), may hold values from 0 to 1
Outputs:
- left: bfloat16 [8, 32768, 128], P('head', ('batch', 'seq')), parts along dimension 1
- right: float32 [32, 128, 128], P(('batch', 'head')), parts along dimension 0
There are 4 independent parts, one for each index of `batch`. A program takes and returns all parts, laid end to end along the dimension named above; an argument that names none is the same for every part. Nothing has to cross between parts.
All inputs are finite; a program needn't handle non-finite values. No bound on the sum of `outlier` on one device may be relied on, other than what follows from the above.
Results may differ from a plain program's by a relative error of at most 0.0015.
Values sent between devices are 32-bit elements; how exact they have to be, the bound alone decides.
No kernel may reach another device: no remote copies, remote signals or barrier semaphores. Data moves between devices by JAX's collectives and lax.ppermute only.
A program may use at most 192 MiB of HBM per device.

v0:
```python
import math
import jax
import jax.numpy as jnp
from jax import lax
from jax.sharding import PartitionSpec as P

ITERS = 2
complete_cycle = 2.0 * math.pi


def shards(hidden, row_scale, key_value_weight, outlier, sketch_sign_flags):
    tok_rows = hidden.shape[0]
    head_count = key_value_weight.shape[1]
    kv_cols = key_value_weight.shape[2]
    head_dim = kv_cols // 2
    rank_cols = sketch_sign_flags.shape[3]
    group_count = outlier.shape[0]
    highest = lax.Precision.HIGHEST
    weight_piece = lax.all_gather(key_value_weight, "seq", axis=0, tiled=True)
    flat_piece = weight_piece.reshape(weight_piece.shape[0], head_count * kv_cols)
    projected_key_value = jnp.dot(hidden, flat_piece, precision=highest)
    projected_key_value = projected_key_value * row_scale[:, None]
    grouped_rows = projected_key_value.reshape(
        group_count, tok_rows // group_count, head_count, kv_cols
    )
    quantization_spacing = jnp.max(jnp.abs(grouped_rows), axis=1, keepdims=True) / 7.0 + 1e-06
    retain_mask = (1 - outlier).astype(jnp.float32)[:, None, :, None]
    residual_error = (
        retain_mask * jnp.sin(complete_cycle * grouped_rows / quantization_spacing)
    ).reshape(tok_rows, head_count, 2, head_dim)
    sign_matrix = (2 * sketch_sign_flags - 1).astype(jnp.float32)
    sketch = jnp.einsum("thec,heck->thek", residual_error, sign_matrix, precision=highest)
    for iteration in range(ITERS):
        local_gram = jnp.einsum("thek,theq->hekq", sketch, sketch, precision=highest)
        gram_matrix = lax.psum(local_gram, "seq")
        lower_factor = jnp.linalg.cholesky(gram_matrix)
        identity = jnp.broadcast_to(jnp.eye(rank_cols, dtype=gram_matrix.dtype), gram_matrix.shape)
        inverse_factor = jax.scipy.linalg.solve_triangular(lower_factor, identity, lower=True)
        basis_matrix = jnp.einsum("thek,heqk->theq", sketch, inverse_factor, precision=highest)
        local_coef = jnp.einsum("thec,theq->hecq", residual_error, basis_matrix, precision=highest)
        coefficient_rows = lax.psum(local_coef, "seq")
        if iteration + 1 < ITERS:
            sketch = jnp.einsum(
                "thec,hecq->theq", residual_error, coefficient_rows, precision=highest
            )
    root_length = math.sqrt(tok_rows * lax.axis_size("seq"))
    left = (
        (root_length * basis_matrix)
        .transpose(1, 0, 2, 3)
        .reshape(head_count, tok_rows, 2 * rank_cols)
        .astype(jnp.bfloat16)
    )
    right = (
        (coefficient_rows / root_length)
        .transpose(0, 2, 1, 3)
        .reshape(head_count, head_dim, 2 * rank_cols)
    )
    return (left, right)


def solution(mesh):
    return jax.shard_map(
        shards,
        mesh=mesh,
        in_specs=(
            P(("batch", "seq"), None),
            P(("batch", "seq")),
            P("seq", "head", None),
            P(("batch", "seq"), "head"),
            P("head", None, None, None),
        ),
        out_specs=(P("head", ("batch", "seq"), None), P(("batch", "head"), None, None)),
        check_vma=False,
    )
```

profile of v0, /device:TPU:0, one launch (start us, length us, event | category | flops | bytes accessed | tf_op | source)
XLA Modules:
  0.0 858.8 jit_solution(14637617141155702260)
XLA Ops:
  8.1 201.4 %all-gather.2.cloned.1.call-done = f32[8192,4,256]{2,1,0:T(4,128)} async-done(((f32[512,4,256]{2,1,0:T(4,128)}), f32[8192,4,256]{2,1,0:T(4,128)}) %all-gather.2.cloned.1.call-update) | async-done | bytes 33554448 | tf_op jit(solution)/shard_map/all_gather | solution.py:19
  209.6 27.5 %copy.108 = f32[1024,8,4,256]{3,1,2,0:T(8,128)} copy(f32[1024,8,4,256]{3,2,1,0:T(4,128)} %bitcast.58) | data formatting | bytes 67108864
  237.1 60.5 %multiply_abs_fusion = (f32[512,1024]{1,0:T(8,128)}, f32[512,1024]{1,0:T(8,128)}) fusion(f32[512]{0:T(512)S(1)} %copy-done.3, f32[512,8192]{1,0:T(8,128)} %param.8, f32[8192,1024]{1,0:T(8,128)} %bitcast.59), kind=kOutput, calls=%fused_computation.3 | convolution fusion | flops 51541180416 | bytes 54528000 | tf_op jit(solution)/shard_map/dot_general | solution.py:21
  297.6 2.2 abs.7
  300.3 2.1 div.32
  302.4 1.9 copy.86
  304.4 1.8 copy.88
  306.2 8.9 %fusion.1 = f32[512,4,2,128]{3,0,2,1:T(8,128)S(1)} fusion(f32[512,4,2,128]{3,0,2,1:T(8,128)} %copy.88, f32[512,4,2,128]{3,2,0,1:T(2,128)} %div.32, f32[512,4]{0,1:T(4,128)S(1)} %mul.46), kind=kLoop, calls=%fused_computation.2 | loop fusion | flops 1048576 | bytes 6299648 | tf_op jit(solution)/shard_map/mul | solution.py:29
  315.1 2.4 convolution_bitcast_fusion.1
  317.5 1.8 fusion.21
  319.4 83.9 %all-reduce.5.cloned.1.call-done = f32[4,2,64,64]{2,3,1,0:T(8,128)} async-done(((f32[4,2,64,64]{2,3,1,0:T(8,128)}), f32[4,2,64,64]{2,3,1,0:T(8,128)}) %all-reduce.5.cloned.1.call-update) | async-done | bytes 131088 | tf_op jit(solution)/shard_map/psum | solution.py:35
  403.3 1.1 copy.91
  404.3 1.7 fusion.9
  406.0 47.6 %custom-call.8 = f32[4,2,64,64]{3,2,1,0:T(8,128)S(1)} custom-call(f32[4,2,64,64]{3,2,1,0:T(8,128)} %fusion.9), custom_call_target="Cholesky" | custom-call | tf_op jit(solution)/shard_map/jit(cholesky)/cholesky | solution.py:36
  453.8 0.8 select_bitcast_fusion.1
  454.7 40.0 %custom-call.9 = f32[4,2,1,64,64]{3,4,2,1,0:T(8,128)S(1)} custom-call(f32[4,2,1,64,64]{4,3,2,1,0:T(8,128)} %select_bitcast_fusion.1), custom_call_target="InvertDiagBlocksLowerTriangular" | custom-call | tf_op jit(solution)/shard_map/jit(_solve_triangular)/vmap(vmap())/triangular_solve | solution.py:38
  495.3 1.0 convolution_bitcast_fusion.2
  496.3 2.2 fusion.22
  498.6 83.5 %all-reduce.7.cloned.1.call-done = f32[4,2,128,64]{2,3,1,0:T(8,128)} async-done(((f32[4,2,128,64]{2,3,1,0:T(8,128)}), f32[4,2,128,64]{2,3,1,0:T(8,128)}) %all-reduce.7.cloned.1.call-update) | async-done | bytes 262160 | tf_op jit(solution)/shard_map/psum | solution.py:41
  582.1 3.3 convolution_bitcast_fusion
  585.4 1.8 fusion.23
  587.3 83.6 %all-reduce.9.cloned.1.call-done = f32[4,2,64,64]{2,3,1,0:T(8,128)} async-done(((f32[4,2,64,64]{2,3,1,0:T(8,128)}), f32[4,2,64,64]{2,3,1,0:T(8,128)}) %all-reduce.9.cloned.1.call-update) | async-done | bytes 131088 | tf_op jit(solution)/shard_map/psum | solution.py:35
  670.8 1.1 copy.96
  671.9 1.7 fusion.6
  673.6 47.6 %custom-call.10 = f32[4,2,64,64]{3,2,1,0:T(8,128)S(1)} custom-call(f32[4,2,64,64]{3,2,1,0:T(8,128)} %fusion.6), custom_call_target="Cholesky" | custom-call | tf_op jit(solution)/shard_map/jit(cholesky)/cholesky | solution.py:36
  722.2 40.0 %custom-call.11 = f32[4,2,1,64,64]{3,4,2,1,0:T(8,128)S(1)} custom-call(f32[4,2,1,64,64]{4,3,2,1,0:T(8,128)} %select_bitcast_fusion), custom_call_target="InvertDiagBlocksLowerTriangular" | custom-call | tf_op jit(solution)/shard_map/jit(_solve_triangular)/vmap(vmap())/triangular_solve | solution.py:38
  762.9 1.8 multiply_convert_fusion
  764.7 2.2 fusion.2
  766.9 1.0 copy.100
  767.9 82.5 %all-reduce.11.cloned.1.call-done = f32[4,2,128,64]{2,3,1,0:T(8,128)} async-done(((f32[4,2,128,64]{2,3,1,0:T(8,128)}), f32[4,2,128,64]{2,3,1,0:T(8,128)}) %all-reduce.11.cloned.1.call-update) | async-done | bytes 262160 | tf_op jit(solution)/shard_map/psum | solution.py:41
  850.5 1.0 broadcast_multiply_fusion
  851.4 0.8 copy.101
  (34 shorter events, 4.0 us)
Async XLA Ops:
  7.2 0.8 copy-start.2
  7.2 202.4 %all-gather.2.cloned.1.call-start = ((), (), s32[]{:S(2)}) async-start(), calls=%async_computation | async-start | bytes 35651584 | tf_op jit(solution)/shard_map/all_gather | solution.py:19
  7.9 395.4 %all-reduce.5.cloned.1.call-start = ((), (), s32[]{:S(2)}) async-start(), calls=%async_computation.1 | async-start | bytes 524288 | tf_op jit(solution)/shard_map/psum | solution.py:35
  209.6 27.5 %copy-start.3 = (f32[512]{0:T(512)S(1)}, f32[512]{0:T(512)}, u32[]{:S(2)}) copy-start(f32[512]{0:T(512)} %param.9) | copy-start | bytes 6148
  306.2 8.9 %copy-start.1 = (s32[4,2,128,64]{2,3,1,0:T(8,128)S(1)}, s32[4,2,128,64]{2,3,1,0:T(8,128)}, u32[]{:S(2)}) copy-start(s32[4,2,128,64]{2,3,1,0:T(8,128)} %param.12) | copy-start | bytes 786436
  319.3 262.8 %all-reduce.7.cloned.1.call-start = ((), (), s32[]{:S(2)}) async-start(), calls=%async_computation.2 | async-start | bytes 524288 | tf_op jit(solution)/shard_map/psum | solution.py:41
  498.6 172.3 %all-reduce.9.cloned.1.call-start = ((), (), s32[]{:S(2)}) async-start(), calls=%async_computation.3 | async-start | bytes 524288 | tf_op jit(solution)/shard_map/psum | solution.py:35
  587.2 263.2 %all-reduce.11.cloned.1.call-start = ((), (), s32[]{:S(2)}) async-start(), calls=%async_computation.4 | async-start | bytes 524288 | tf_op jit(solution)/shard_map/psum | solution.py:41
  764.7 2.3 copy-start
Sparse Core Ops, SparseCore 0:
  10.1 199.3 all-gather.1
  319.4 83.7 all-reduce.4
  498.7 83.3 all-reduce.6
  587.3 83.4 all-reduce.8
  767.1 83.3 all-reduce.10
where the time goes:
time: 860 us; the launch traced here: 859 us
  waiting for transfers between devices  536 us (62%)
  other arithmetic  191 us (22%)
  matrix products  78.2 us (9%)
  local copies, waits for them, and re-layouts  39.9 us (5%)
  between operations  14 us (2%)
    all_gather x1, waiting for transfers between devices, shards(): weight_piece = lax.all_gather(key_value_weight, 'seq', axis=0, tiled=True)  201 us
    psum x2, waiting for transfers between devices, shards(): gram_matrix = lax.psum(local_gram, 'seq')  167 us
    psum x2, waiting for transfers between devices, shards(): coefficient_rows = lax.psum(local_coef, 'seq')  166 us
    another operation x7, other arithmetic, shards(): lower_factor = jnp.linalg.cholesky(gram_matrix)  95.6 us
    another operation x5, other arithmetic, shards(): jax.scipy.linalg.solve_triangular(lower_factor, identity, lower=True)  81.7 us
    dot_general x1, matrix products, shards(): projected_key_value = jnp.dot(hidden, flat_piece, precision=highest)  60.5 us
    unnamed x11, local copies, waits for them, and re-layouts  29.4 us
  transfers between devices with their start and end apart: 5, of which 5 were waited for; matrix products, arithmetic and copies ran while one was open for 0% of the time, Pallas kernels for 0%

commit v1 on v0

--- a/solution.py
+++ b/solution.py
@@ -6,6 +6,18 @@
 
 ITERS = 2
 complete_cycle = 2.0 * math.pi
+
+
+def return_all_the_seats_all(panel):
+    num = jax.lax.axis_size("seq")
+    x_new = panel
+    for c in [d for d in (1, 2, 4, 8, 16) if d < num]:
+        bank = []
+        for t in [*range(num)]:
+            bank.append((t, t ^ c))
+        high = jax.lax.ppermute(x_new, "seq", bank)
+        x_new = x_new + high
+    return x_new
 
 
 def shards(hidden, row_scale, key_value_weight, outlier, sketch_sign_flags):
@@ -38,7 +50,7 @@
         inverse_factor = jax.scipy.linalg.solve_triangular(lower_factor, identity, lower=True)
         basis_matrix = jnp.einsum("thek,heqk->theq", sketch, inverse_factor, precision=highest)
         local_coef = jnp.einsum("thec,theq->hecq", residual_error, basis_matrix, precision=highest)
-        coefficient_rows = lax.psum(local_coef, "seq")
+        coefficient_rows = return_all_the_seats_all(local_coef)
         if iteration + 1 < ITERS:
             sketch = jnp.einsum(
                 "thec,hecq->theq", residual_error, coefficient_rows, precision=highest

time: 860 us -> 752 us (0.87)
  waiting for transfers between devices: 536 us -> 422 us
  starting transfers between devices: 0.2 us -> 9.17 us
    psum x2 -> x0, waiting for transfers between devices: 166 us -> none  [shards(): coefficient_rows = lax.psum(local_coef, 'seq')]
    ppermute x0 -> x8, waiting for transfers between devices: none -> 52.5 us  [return_all_the_seats_all(): high = jax.lax.ppermute(x_new, 'seq', bank)]
    ppermute x0 -> x8, starting transfers between devices: none -> 9.05 us  [return_all_the_seats_all(): high = jax.lax.ppermute(x_new, 'seq', bank)]
  transfers between devices with their start and end apart: 5 -> 11, of which waited for: 5 -> 11; matrix products, arithmetic and copies ran while one was open for 0% -> 0% of each run, Pallas kernels for 0% -> 0%
where the time goes in v1:
time: 752 us; the launch traced here: 751 us
  waiting for transfers between devices  422 us (56%)
  other arithmetic  190 us (25%)
  matrix products  76 us (10%)
  local copies, waits for them, and re-layouts  39.9 us (5%)
  between operations  14 us (2%)
  starting transfers between devices  9.17 us (1%)
    all_gather x1, waiting for transfers between devices, shards(): weight_piece = lax.all_gather(key_value_weight, 'seq', axis=0, tiled=True)  201 us
    psum x2, waiting for transfers between devices, shards(): gram_matrix = lax.psum(local_gram, 'seq')  167 us
    another operation x7, other arithmetic, shards(): lower_factor = jnp.linalg.cholesky(gram_matrix)  95.6 us
    another operation x5, other arithmetic, shards(): jax.scipy.linalg.solve_triangular(lower_factor, identity, lower=True)  81.7 us
    dot_general x1, matrix products, shards(): projected_key_value = jnp.dot(hidden, flat_piece, precision=highest)  60.5 us
    ppermute x8, waiting for transfers between devices, return_all_the_seats_all(): high = jax.lax.ppermute(x_new, 'seq', bank)  52.5 us
    unnamed x11, local copies, waits for them, and re-layouts  29.4 us
  transfers between devices with their start and end apart: 11, of which 11 were waited for; matrix products, arithmetic and copies ran while one was open for 0% of the time, Pallas kernels for 0%

profile of v1, /device:TPU:0, one launch (start us, length us, event | category | flops | bytes accessed | tf_op | source)
XLA Modules:
  0.0 751.1 jit_solution(3472407862824462253)
XLA Ops:
  8.1 201.4 %all-gather.2.cloned.1.call-done = f32[8192,4,256]{2,1,0:T(4,128)} async-done(((f32[512,4,256]{2,1,0:T(4,128)}), f32[8192,4,256]{2,1,0:T(4,128)}) %all-gather.2.cloned.1.call-update) | async-done | bytes 33554448 | tf_op jit(solution)/shard_map/all_gather | solution.py:31
  209.6 27.5 %copy.109 = f32[1024,8,4,256]{3,1,2,0:T(8,128)} copy(f32[1024,8,4,256]{3,2,1,0:T(4,128)} %bitcast.57) | data formatting | bytes 67108864
  237.1 60.5 %multiply_abs_fusion = (f32[512,1024]{1,0:T(8,128)}, f32[512,1024]{1,0:T(8,128)}) fusion(f32[512]{0:T(512)S(1)} %copy-done.3, f32[512,8192]{1,0:T(8,128)} %param.8, f32[8192,1024]{1,0:T(8,128)} %bitcast.58), kind=kOutput, calls=%fused_computation.3 | convolution fusion | flops 51541180416 | bytes 54528000 | tf_op jit(solution)/shard_map/dot_general | solution.py:33
  297.6 2.2 abs.7
  300.3 2.1 div.32
  302.4 1.9 copy.87
  304.4 1.8 copy.89
  306.2 8.9 %fusion.1 = f32[512,4,2,128]{3,0,2,1:T(8,128)S(1)} fusion(f32[512,4,2,128]{3,0,2,1:T(8,128)} %copy.89, f32[512,4,2,128]{3,2,0,1:T(2,128)} %div.32, f32[512,4]{0,1:T(4,128)S(1)} %mul.46), kind=kLoop, calls=%fused_computation.2 | loop fusion | flops 1048576 | bytes 6299648 | tf_op jit(solution)/shard_map/mul | solution.py:41
  315.1 2.4 convolution_bitcast_fusion.1
  317.5 1.8 fusion.22
  319.4 83.8 %all-reduce.3.cloned.1.call-done = f32[4,2,64,64]{2,3,1,0:T(8,128)} async-done(((f32[4,2,64,64]{2,3,1,0:T(8,128)}), f32[4,2,64,64]{2,3,1,0:T(8,128)}) %all-reduce.3.cloned.1.call-update) | async-done | bytes 131088 | tf_op jit(solution)/shard_map/psum | solution.py:47
  404.3 1.7 fusion.9
  406.0 47.6 %custom-call.8 = f32[4,2,64,64]{3,2,1,0:T(8,128)S(1)} custom-call(f32[4,2,64,64]{3,2,1,0:T(8,128)} %fusion.9), custom_call_target="Cholesky" | custom-call | tf_op jit(solution)/shard_map/jit(cholesky)/cholesky | solution.py:48
  454.6 40.0 %custom-call.9 = f32[4,2,1,64,64]{3,4,2,1,0:T(8,128)S(1)} custom-call(f32[4,2,1,64,64]{4,3,2,1,0:T(8,128)} %select_bitcast_fusion.1), custom_call_target="InvertDiagBlocksLowerTriangular" | custom-call | tf_op jit(solution)/shard_map/jit(_solve_triangular)/vmap(vmap())/triangular_solve | solution.py:50
  496.2 1.6 fusion.23
  499.1 5.6 collective-permute-done
  504.8 1.6 collective-permute-start.1
  506.4 6.4 collective-permute-done.1
  513.7 7.4 collective-permute-done.2
  522.0 7.2 collective-permute-done.3
  529.3 2.4 convolution_bitcast_fusion
  531.6 1.8 fusion.24
  533.4 83.4 %all-reduce.5.cloned.1.call-done = f32[4,2,64,64]{2,3,1,0:T(8,128)} async-done(((f32[4,2,64,64]{2,3,1,0:T(8,128)}), f32[4,2,64,64]{2,3,1,0:T(8,128)}) %all-reduce.5.cloned.1.call-update) | async-done | bytes 131088 | tf_op jit(solution)/shard_map/psum | solution.py:47
  617.9 1.7 fusion.6
  619.6 47.6 %custom-call.10 = f32[4,2,64,64]{3,2,1,0:T(8,128)S(1)} custom-call(f32[4,2,64,64]{3,2,1,0:T(8,128)} %fusion.6), custom_call_target="Cholesky" | custom-call | tf_op jit(solution)/shard_map/jit(cholesky)/cholesky | solution.py:48
  668.2 40.0 %custom-call.11 = f32[4,2,1,64,64]{3,4,2,1,0:T(8,128)S(1)} custom-call(f32[4,2,1,64,64]{4,3,2,1,0:T(8,128)} %select_bitcast_fusion), custom_call_target="InvertDiagBlocksLowerTriangular" | custom-call | tf_op jit(solution)/shard_map/jit(_solve_triangular)/vmap(vmap())/triangular_solve | solution.py:50
  708.9 1.8 multiply_convert_fusion
  710.6 1.6 fusion.2
  713.5 5.7 collective-permute-done.4
  720.8 6.4 collective-permute-done.5
  728.1 7.6 %collective-permute-done.6 = f32[4,2,128,64]{2,3,1,0:T(8,128)S(1)} collective-permute-done((f32[4,2,128,64]{2,3,1,0:T(8,128)S(1)}, f32[4,2,128,64]{2,3,1,0:T(8,128)S(1)}, u32[]{:S(2)}, u32[]{:S(2)}) %collective-permute-start.6) | collective-permute-done | bytes 262176 | tf_op jit(solution)/shard_map/ppermute | solution.py:18
  737.5 6.2 collective-permute-done.7
  (50 shorter events, 17.3 us)
Async XLA Ops:
  7.2 0.8 copy-start.2
  7.2 202.4 %all-gather.2.cloned.1.call-start = ((), (), s32[]{:S(2)}) async-start(), calls=%async_computation | async-start | bytes 35651584 | tf_op jit(solution)/shard_map/all_gather | solution.py:31
  7.9 395.3 %all-reduce.3.cloned.1.call-start = ((), (), s32[]{:S(2)}) async-start(), calls=%async_computation.1 | async-start | bytes 524288 | tf_op jit(solution)/shard_map/psum | solution.py:47
  209.6 27.6 %copy-start.3 = (f32[512]{0:T(512)S(1)}, f32[512]{0:T(512)}, u32[]{:S(2)}) copy-start(f32[512]{0:T(512)} %param.9) | copy-start | bytes 6148
  306.2 8.9 %copy-start.1 = (s32[4,2,128,64]{2,3,1,0:T(8,128)S(1)}, s32[4,2,128,64]{2,3,1,0:T(8,128)}, u32[]{:S(2)}) copy-start(s32[4,2,128,64]{2,3,1,0:T(8,128)} %param.12) | copy-start | bytes 786436
  319.3 297.5 %all-reduce.5.cloned.1.call-start = ((), (), s32[]{:S(2)}) async-start(), calls=%async_computation.2 | async-start | bytes 524288 | tf_op jit(solution)/shard_map/psum | solution.py:47
  497.9 6.9 collective-permute-start
  504.8 8.0 %collective-permute-start.1 = (f32[4,2,128,64]{2,3,1,0:T(8,128)S(1)}, f32[4,2,128,64]{2,3,1,0:T(8,128)S(1)}, u32[]{:S(2)}, u32[]{:S(2)}) collective-permute-start(f32[4,2,128,64]{2,3,1,0:T(8,128)S(1)} %add.51), channel_id=1, source_target_pairs={{0,2},{1,3},{2,0},{3,1},{4,6},{5,7},{6,4},{7,5},{8,10},{9,11},{10,... | collective-permute-start | bytes 786440 | tf_op jit(solution)/shard_map/ppermute | solution.py:18
  512.8 8.3 %collective-permute-start.2 = (f32[4,2,128,64]{2,3,1,0:T(8,128)S(1)}, f32[4,2,128,64]{2,3,1,0:T(8,128)S(1)}, u32[]{:S(2)}, u32[]{:S(2)}) collective-permute-start(f32[4,2,128,64]{2,3,1,0:T(8,128)S(1)} %add.52), channel_id=1, source_target_pairs={{0,4},{1,5},{2,6},{3,7},{4,0},{5,1},{6,2},{7,3},{8,12},{9,13},{10,... | collective-permute-start | bytes 786440 | tf_op jit(solution)/shard_map/ppermute | solution.py:18
  521.1 8.2 %collective-permute-start.3 = (f32[4,2,128,64]{2,3,1,0:T(8,128)S(1)}, f32[4,2,128,64]{2,3,1,0:T(8,128)S(1)}, u32[]{:S(2)}, u32[]{:S(2)}) collective-permute-start(f32[4,2,128,64]{2,3,1,0:T(8,128)S(1)} %add.53), channel_id=1, source_target_pairs={{0,8},{1,9},{2,10},{3,11},{4,12},{5,13},{6,14},{7,15},{8,0},{9,1},... | collective-permute-start | bytes 786440 | tf_op jit(solution)/shard_map/ppermute | solution.py:18
  710.6 25.8 %copy-start = (bf16[4,2,64,512]{3,2,1,0:T(8,128)(2,1)S(1)}, bf16[4,2,64,512]{3,2,1,0:T(8,128)(2,1)}, u32[]{:S(2)}) copy-start(bf16[4,2,64,512]{3,2,1,0:T(8,128)(2,1)} %get-tuple-element.20) | copy-start | bytes 1572868
  712.3 6.9 collective-permute-start.4
  719.2 8.0 %collective-permute-start.5 = (f32[4,2,128,64]{2,3,1,0:T(8,128)S(1)}, f32[4,2,128,64]{2,3,1,0:T(8,128)S(1)}, u32[]{:S(2)}, u32[]{:S(2)}) collective-permute-start(f32[4,2,128,64]{2,3,1,0:T(8,128)S(1)} %add.55), channel_id=1, source_target_pairs={{0,2},{1,3},{2,0},{3,1},{4,6},{5,7},{6,4},{7,5},{8,10},{9,11},{10,... | collective-permute-start | bytes 786440 | tf_op jit(solution)/shard_map/ppermute | solution.py:18
  727.2 8.5 %collective-permute-start.6 = (f32[4,2,128,64]{2,3,1,0:T(8,128)S(1)}, f32[4,2,128,64]{2,3,1,0:T(8,128)S(1)}, u32[]{:S(2)}, u32[]{:S(2)}) collective-permute-start(f32[4,2,128,64]{2,3,1,0:T(8,128)S(1)} %add.56), channel_id=1, source_target_pairs={{0,4},{1,5},{2,6},{3,7},{4,0},{5,1},{6,2},{7,3},{8,12},{9,13},{10,... | collective-permute-start | bytes 786440 | tf_op jit(solution)/shard_map/ppermute | solution.py:18
  735.7 8.0 %collective-permute-start.7 = (f32[4,2,128,64]{2,3,1,0:T(8,128)S(1)}, f32[4,2,128,64]{2,3,1,0:T(8,128)S(1)}, u32[]{:S(2)}, u32[]{:S(2)}) collective-permute-start(f32[4,2,128,64]{2,3,1,0:T(8,128)S(1)} %add.57), channel_id=1, source_target_pairs={{0,8},{1,9},{2,10},{3,11},{4,12},{5,13},{6,14},{7,15},{8,0},{9,1},... | collective-permute-start | bytes 786440 | tf_op jit(solution)/shard_map/ppermute | solution.py:18
Sparse Core Ops, SparseCore 0:
  10.1 199.3 all-gather.1
  319.4 83.7 all-reduce.2
  533.5 83.2 all-reduce.4
